TPU v7x, 256 devices: a whole 4x4x8 slice. The times are simulated.
256 devices in a mesh: gx: 64 (over z, x, core), gy: 4 (over y).
Axes of the slice: x: 4, y: 4, z: 8, core: 2. Of those that a mesh axis runs over, the one named last changes fastest.
Arguments:
- pressure: float32 [512, 512, 128], P('gx', 'gy'), may hold values from -6 to 8
- vel_y: float32 [512, 512, 128], P('gx', 'gy'), may hold values from -6 to 6
- vel_z: float32 [512, 512, 128], P('gx', 'gy'), may hold values from -6 to 6
- material: int32 [512, 512, 128], P('gx', 'gy'), may hold values from 0 to 7
- absorb_table: float32 [8], replicated, may hold values from 0.02 to 4
Outputs:
- pressure_next: float32 [512, 512, 128], P('gx', 'gy')
- vel_y_next: float32 [512, 512, 128], P('gx', 'gy')
- vel_z_next: float32 [512, 512, 128], P('gx', 'gy')
All inputs are finite; a program needn't handle non-finite values.
Results may differ from a plain program's by a relative error of at most 0.0004.
Values sent between devices are 32-bit elements; how exact they have to be, the bound alone decides.
A program may use at most 128 MiB of HBM per device.

v0:
```python
import jax
import jax.numpy as jnp
from jax import lax
from jax.sharding import PartitionSpec as P

MATS = 8


def passed_along(value, axis, steps):
    count = lax.axis_size(axis)
    first, last = (max(0, -steps), min(count, count - steps))
    return lax.ppermute(value, axis, [(source, source + steps) for source in range(first, last)])


def join_segments(left, right):
    denom = 1.0 - left[5] * right[1]
    inner_const = (left[3] + left[5] * right[0]) / denom
    inner_left = left[4] / denom
    inner_right = left[5] * right[2] / denom
    outer_const = right[0] + right[1] * inner_const
    outer_left = right[1] * inner_left
    outer_right = right[2] + right[1] * inner_right
    return (
        left[0] + left[2] * outer_const,
        left[1] + left[2] * outer_left,
        left[2] * outer_right,
        right[3] + right[4] * inner_const,
        right[4] * inner_left,
        right[5] + right[4] * inner_right,
    )


def sweep_lines(excess, stacked):

    def forward(carry, items):
        carried, value_prev = carry
        excess_row, value_row = items
        inverse = 1.0 / (1.0 + excess_row + carried)
        value = (value_row + value_prev) * inverse[None]
        carried_next = (excess_row + carried) * inverse
        return ((carried_next, value), (inverse, value))

    start = (jnp.ones(excess.shape[1:], jnp.float32), jnp.zeros(stacked.shape[1:], jnp.float32))
    _, (inverses, values) = lax.scan(forward, start, (excess, stacked))

    def backward(following, items):
        inverse, value = items
        current = value + inverse[None] * following
        return (current, current)

    _, solved = lax.scan(
        backward, jnp.zeros(stacked.shape[1:], jnp.float32), (inverses, values), reverse=True
    )
    return solved


def body(pressure, vel_y, vel_z, material, absorb_table):
    absorb = jnp.zeros(pressure.shape, jnp.float32)
    for entry in range(MATS):
        absorb = absorb + jnp.where(material == entry, absorb_table[entry], 0.0)
    damping = 1.0 / (1.0 + absorb)
    above = passed_along(pressure[:, :1, :], "gy", -1)
    upper_y = jnp.concatenate([pressure[:, 1:, :], above], axis=1)
    upper_z = jnp.concatenate([pressure[:, :, 1:], jnp.zeros_like(pressure[:, :, :1])], axis=2)
    vel_y_next = damping * (vel_y - 0.5 * (upper_y - pressure))
    vel_z_next = damping * (vel_z - 0.5 * (upper_z - pressure))
    below = passed_along(vel_y_next[:, -1:, :], "gy", 1)
    lower_y = jnp.concatenate([below, vel_y_next[:, :-1, :]], axis=1)
    lower_z = jnp.concatenate([jnp.zeros_like(pressure[:, :, :1]), vel_z_next[:, :, :-1]], axis=2)
    source = pressure - 0.5 * (vel_y_next - lower_y + vel_z_next - lower_z)
    line_cells = pressure.shape[0] * lax.axis_size("gx")
    coupling = 1.0 * (line_cells * line_cells // 4)
    excess = (1.0 + absorb) / coupling
    scaled = source / coupling
    rows = lax.broadcasted_iota(jnp.int32, pressure.shape, 0)
    first_unit = jnp.where(rows == 0, -1.0, 0.0)
    last_unit = jnp.where(rows == pressure.shape[0] - 1, -1.0, 0.0)
    stacked = jnp.stack([scaled, first_unit, last_unit], axis=1)
    solved = sweep_lines(excess, stacked)
    local_part = solved[:, 0]
    left_spike = solved[:, 1]
    right_spike = solved[:, 2]
    own = (
        local_part[0],
        -left_spike[0],
        -right_spike[0],
        local_part[-1],
        -left_spike[-1],
        -right_spike[-1],
    )
    nothing = jnp.zeros(local_part.shape[1:], jnp.float32)
    single = jnp.ones(local_part.shape[1:], jnp.float32)
    identity = (nothing, nothing, single, nothing, single, nothing)
    table = (
        lax.all_gather(own[0][None], "gx", axis=0, tiled=True),
        lax.all_gather(own[1][None], "gx", axis=0, tiled=True),
        lax.all_gather(own[2][None], "gx", axis=0, tiled=True),
        lax.all_gather(own[3][None], "gx", axis=0, tiled=True),
        lax.all_gather(own[4][None], "gx", axis=0, tiled=True),
        lax.all_gather(own[5][None], "gx", axis=0, tiled=True),
    )
    position = lax.axis_index("gx")
    indices = jnp.arange(lax.axis_size("gx"), dtype=jnp.int32)

    def take_lower(carry, items):
        index, pieces = items
        merged = join_segments(carry, pieces)
        keep = index < position
        return (tuple((jnp.where(keep, fresh, older) for fresh, older in zip(merged, carry))), None)

    def take_higher(carry, items):
        index, pieces = items
        merged = join_segments(pieces, carry)
        keep = index > position
        return (tuple((jnp.where(keep, fresh, older) for fresh, older in zip(merged, carry))), None)

    prefix, _ = lax.scan(take_lower, identity, (indices, table))
    suffix, _ = lax.scan(take_higher, identity, (indices, table), reverse=True)
    top_rhs = own[0] + own[1] * prefix[3] + own[2] * suffix[0]
    bottom_rhs = own[3] + own[4] * prefix[3] + own[5] * suffix[0]
    top_top = 1.0 - own[1] * prefix[5]
    top_bottom = -own[2] * suffix[1]
    bottom_top = -own[4] * prefix[5]
    bottom_bottom = 1.0 - own[5] * suffix[1]
    determinant = top_top * bottom_bottom - top_bottom * bottom_top
    top_value = (top_rhs * bottom_bottom - top_bottom * bottom_rhs) / determinant
    bottom_value = (top_top * bottom_rhs - bottom_top * top_rhs) / determinant
    before_value = prefix[3] + prefix[5] * top_value
    after_value = suffix[0] + suffix[1] * bottom_value
    pressure_next = local_part - left_spike * before_value[None] - right_spike * after_value[None]
    return (pressure_next, vel_y_next, vel_z_next)


def solution(mesh):
    return jax.shard_map(
        body,
        mesh=mesh,
        in_specs=(
            P("gx", "gy", None),
            P("gx", "gy", None),
            P("gx", "gy", None),
            P("gx", "gy", None),
            P(),
        ),
        out_specs=(P("gx", "gy", None), P("gx", "gy", None), P("gx", "gy", None)),
        check_vma=False,
    )
```

profile of v0, /device:TPU:1, one launch (start us, length us, event | category | flops | bytes accessed | tf_op | source)
XLA Modules:
  0.0 848.9 jit_solution(11246831425350953470)
XLA Ops:
  8.1 1.3 collective-permute-start
  9.4 1.6 fusion.49
  11.0 1.1 slice.93
  12.1 1.2 slice.97
  13.4 6.4 fusion.32
  19.8 4.6 collective-permute-start.1
  25.8 1.4 broadcast.68.clone
  27.2 20.3 %while.64 = (s32[]{:T(128)}, f32[128,128]{1,0:T(8,128)S(1)}, f32[3,128,128]{2,1,0:T(8,128)S(1)}, f32[8,128,128]{2,1,0:T(8,128)S(1)}, f32[8,3,128,128]{3,2,1,0:T(...) while((s32[]{:T(128)}, f32[128,128]{1,0:T(8,128)S(1)}, ...), condition=%wide.region_1.2_spmd.clone, body=%wide.region_0.1_spmd.clone.sunk | while | flops 262147 | bytes 1376881 | solution.py:44
  48.5 15.2 %while.65 = (s32[]{:T(128)}, f32[3,128,128]{2,1,0:T(8,128)S(1)}, f32[8,3,128,128]{3,2,1,0:T(8,128)S(1)}, f32[8,3,128,128]{3,2,1,0:T(8,128)}, f32[8,128,128]{2,1,0:T(8,128)}, /*index=5*/s32[]{:T(128)}, s32[]{:T(128)}, s32[]{:T(128)}) while((s32[]{:T(128)}, f32[3,128,128]{2,1,0:T(8,128)S(1)}, f32[8,3,128,128]{3,2,1,0:T(8,128)S(1)}, ...), condition=%wide.region_3.4_spmd.clone, body=%wide.region_2.3_spmd.clone.sunk | while | flops 147460 | bytes 983155 | solution.py:51
  67.7 81.3 %all-gather.13.cloned.1.call-done = f32[64,1,128,128]{3,2,1,0:T(8,128)} async-done(((f32[1,1,128,128]{3,2,1,0:T(8,128)}), f32[64,1,128,128]{3,2,1,0:T(8,128)}) %all-gather.13.cloned.1.call-update) | async-done | bytes 4194320 | tf_op jit(solution)/shard_map/all_gather | solution.py:98
  149.1 79.5 %all-gather.15.cloned.1.call-done = f32[64,1,128,128]{3,2,1,0:T(8,128)} async-done(((f32[1,1,128,128]{3,2,1,0:T(8,128)}), f32[64,1,128,128]{3,2,1,0:T(8,128)}) %all-gather.15.cloned.1.call-update) | async-done | bytes 4194320 | tf_op jit(solution)/shard_map/all_gather | solution.py:99
  228.6 79.0 %all-gather.17.cloned.1.call-done = f32[64,1,128,128]{3,2,1,0:T(8,128)} async-done(((f32[1,1,128,128]{3,2,1,0:T(8,128)}), f32[64,1,128,128]{3,2,1,0:T(8,128)}) %all-gather.17.cloned.1.call-update) | async-done | bytes 4194320 | tf_op jit(solution)/shard_map/all_gather | solution.py:95
  307.6 78.8 %all-gather.19.cloned.1.call-done = f32[64,1,128,128]{3,2,1,0:T(8,128)} async-done(((f32[1,1,128,128]{3,2,1,0:T(8,128)}), f32[64,1,128,128]{3,2,1,0:T(8,128)}) %all-gather.19.cloned.1.call-update) | async-done | bytes 4194320 | tf_op jit(solution)/shard_map/all_gather | solution.py:96
  386.4 78.8 %all-gather.21.cloned.1.call-done = f32[64,1,128,128]{3,2,1,0:T(8,128)} async-done(((f32[1,1,128,128]{3,2,1,0:T(8,128)}), f32[64,1,128,128]{3,2,1,0:T(8,128)}) %all-gather.21.cloned.1.call-update) | async-done | bytes 4194320 | tf_op jit(solution)/shard_map/all_gather | solution.py:100
  465.2 78.8 %all-gather.23.cloned.1.call-done = f32[64,1,128,128]{3,2,1,0:T(8,128)} async-done(((f32[1,1,128,128]{3,2,1,0:T(8,128)}), f32[64,1,128,128]{3,2,1,0:T(8,128)}) %all-gather.23.cloned.1.call-update) | async-done | bytes 4194320 | tf_op jit(solution)/shard_map/all_gather | solution.py:97
  544.0 148.7 %while.67 = (s32[]{:T(128)}, f32[128,128]{1,0:T(8,128)S(1)}, f32[128,128]{1,0:T(8,128)S(1)}, s32[64]{0:T(128)S(1)}, s32[]{:T(128)}, /*index=5*/f32[64,128,128]{2...) while((s32[]{:T(128)}, f32[128,128]{1,0:T(8,128)S(1)}, ...), condition=%wide.region_7.8_spmd.clone, body=%wide.region_6.7_spmd.clone.sunk | while | flops 278533 | bytes 655541 | solution.py:118
  545.3 1.1 fusion.56
  547.6 1.1 fusion.56
  549.9 1.1 fusion.56
  552.3 1.1 fusion.56
  554.6 1.1 fusion.56
  556.9 1.1 fusion.56
  559.2 1.1 fusion.56
  561.5 1.1 fusion.56
  563.9 1.1 fusion.56
  566.2 1.1 fusion.56
  568.5 1.1 fusion.56
  570.8 1.1 fusion.56
  573.2 1.1 fusion.56
  575.5 1.1 fusion.56
  577.8 1.1 fusion.56
  580.1 1.1 fusion.56
  582.5 1.1 fusion.56
  584.8 1.1 fusion.56
  587.1 1.1 fusion.56
  589.4 1.1 fusion.56
  591.7 1.1 fusion.56
  594.1 1.1 fusion.56
  596.4 1.1 fusion.56
  598.7 1.1 fusion.56
  601.0 1.1 fusion.56
  603.4 1.1 fusion.56
  605.7 1.1 fusion.56
  608.0 1.1 fusion.56
  610.3 1.1 fusion.56
  612.7 1.1 fusion.56
  615.0 1.1 fusion.56
  692.7 148.3 %while.66 = (s32[]{:T(128)}, f32[128,128]{1,0:T(8,128)S(1)}, f32[128,128]{1,0:T(8,128)S(1)}, s32[64]{0:T(128)S(1)}, s32[]{:T(128)}, /*index=5*/f32[64,128,128]{2...) while((s32[]{:T(128)}, f32[128,128]{1,0:T(8,128)S(1)}, ...), condition=%wide.region_5.6_spmd.clone, body=%wide.region_4.5_spmd.clone.sunk | while | flops 245764 | bytes 655521 | solution.py:117
  (315 shorter events, 221.0 us)
Async XLA Ops:
  7.2 6.2 copy-start
  7.2 6.2 copy-start.4
  7.2 6.2 copy-start.5
  7.2 141.9 %all-gather.13.cloned.1.call-start = ((), (), s32[]{:S(2)}) async-start(), calls=%async_computation | async-start | bytes 4259840 | tf_op jit(solution)/shard_map/all_gather | solution.py:98
  7.2 6.2 copy-start.6
  8.1 5.2 collective-permute-start
  19.8 5.7 copy-start.1
  19.8 5.7 copy-start.2
  19.8 5.4 collective-permute-start.1
  47.5 0.8 copy-start.3
  64.5 164.2 %all-gather.15.cloned.1.call-start = ((), (), s32[]{:S(2)}) async-start(), calls=%async_computation.1 | async-start | bytes 4259840 | tf_op jit(solution)/shard_map/all_gather | solution.py:99
  65.2 242.4 %all-gather.17.cloned.1.call-start = ((), (), s32[]{:S(2)}) async-start(), calls=%async_computation.2 | async-start | bytes 4259840 | tf_op jit(solution)/shard_map/all_gather | solution.py:95
  65.9 320.5 %all-gather.19.cloned.1.call-start = ((), (), s32[]{:S(2)}) async-start(), calls=%async_computation.3 | async-start | bytes 4259840 | tf_op jit(solution)/shard_map/all_gather | solution.py:96
  66.5 398.7 %all-gather.21.cloned.1.call-start = ((), (), s32[]{:S(2)}) async-start(), calls=%async_computation.4 | async-start | bytes 4259840 | tf_op jit(solution)/shard_map/all_gather | solution.py:100
  67.1 476.9 %all-gather.23.cloned.1.call-start = ((), (), s32[]{:S(2)}) async-start(), calls=%async_computation.5 | async-start | bytes 4259840 | tf_op jit(solution)/shard_map/all_gather | solution.py:97
Sparse Core Ops, SparseCore 0:
  64.6 84.4 all-gather.12
  152.4 76.1 all-gather.14
  231.4 76.1 all-gather.16
  310.2 76.1 all-gather.18
  389.0 76.1 all-gather.20
  467.8 76.1 all-gather.22
where the time goes:
time: 859 us; the launch traced here: 849 us
  waiting for transfers between devices  480 us (56%)
  other arithmetic  172 us (20%)
  local copies, waits for them, and re-layouts  89.3 us (10%)
  loops' own time  86.8 us (10%)
  between operations  14.4 us (2%)
    all_gather x1, waiting for transfers between devices, body(): lax.all_gather(own[3][None], 'gx', axis=0, tiled=True)  81.3 us
    all_gather x1, waiting for transfers between devices, body(): lax.all_gather(own[4][None], 'gx', axis=0, tiled=True)  79.5 us
    all_gather x1, waiting for transfers between devices, body(): lax.all_gather(own[0][None], 'gx', axis=0, tiled=True)  79 us
    all_gather x1, waiting for transfers between devices, body(): lax.all_gather(own[2][None], 'gx', axis=0, tiled=True)  78.8 us
    all_gather x1, waiting for transfers between devices, body(): lax.all_gather(own[1][None], 'gx', axis=0, tiled=True)  78.8 us
    all_gather x1, waiting for transfers between devices, body(): lax.all_gather(own[5][None], 'gx', axis=0, tiled=True)  78.8 us
    dynamic_slice x128, local copies, waits for them, and re-layouts, body(): prefix, _ = lax.scan(take_lower, identity, (indices, table))  75.1 us
    select_n x64, other arithmetic, take_higher(): jnp.where(keep, fresh, older)  67.8 us
  transfers between devices with their start and end apart: 8, of which 7 were waited for; matrix products, arithmetic and copies ran while one was open for 0% of the time, Pallas kernels for 0%

commit v1 on v0

--- a/solution.py
+++ b/solution.py
@@ -1,9 +1,19 @@
+import functools
 import jax
 import jax.numpy as jnp
 from jax import lax
 from jax.sharding import PartitionSpec as P
 
 MATS = 8
+
+
+def fill_ports(field_in, a_name, where_dim):
+    out_arr = lax.axis_size(a_name)
+    u_next = jnp.concatenate(out_arr * [field_in], axis=where_dim)
+    return lax.all_to_all(u_next, a_name, where_dim, where_dim, tiled=True)
+
+
+form_scales_now = functools.partial(fill_ports, a_name="gx", where_dim=0)
 
 
 def passed_along(value, axis, steps):
@@ -94,7 +104,7 @@
     table = (
         lax.all_gather(own[0][None], "gx", axis=0, tiled=True),
         lax.all_gather(own[1][None], "gx", axis=0, tiled=True),
-        lax.all_gather(own[2][None], "gx", axis=0, tiled=True),
+        form_scales_now(own[2][None]),
         lax.all_gather(own[3][None], "gx", axis=0, tiled=True),
         lax.all_gather(own[4][None], "gx", axis=0, tiled=True),
         lax.all_gather(own[5][None], "gx", axis=0, tiled=True),

time: 859 us -> 801 us (0.932)
  waiting for transfers between devices: 480 us -> 406 us
  starting transfers between devices: 6.16 us -> 19.8 us
    all_to_all x0 -> x1, waiting for transfers between devices: none -> 106 us  [fill_ports(): return lax.all_to_all(u_next, a_name, where_dim, where_dim, tiled=True)]
    all_gather x1, waiting for transfers between devices: 81.3 us -> 0.01 us  [body(): lax.all_gather(own[3][None], 'gx', axis=0, tiled=True)]
    all_gather x1 -> x0, waiting for transfers between devices: 78.8 us -> none  [body(): lax.all_gather(own[2][None], 'gx', axis=0, tiled=True)]
    all_gather x1, waiting for transfers between devices: 79.5 us -> 60.7 us  [body(): lax.all_gather(own[4][None], 'gx', axis=0, tiled=True)]
    all_to_all x0 -> x1, starting transfers between devices: none -> 13.6 us  [fill_ports(): return lax.all_to_all(u_next, a_name, where_dim, where_dim, tiled=True)]
  transfers between devices with their start and end apart: 8 -> 8, of which waited for: 7 -> 6; matrix products, arithmetic and copies ran while one was open for 0% -> 1% of each run, Pallas kernels for 0% -> 0%
where the time goes in v1:
time: 801 us; the launch traced here: 791 us
  waiting for transfers between devices  406 us (51%)
  other arithmetic  172 us (21%)
  local copies, waits for them, and re-layouts  91.8 us (11%)
  loops' own time  86.8 us (11%)
  starting transfers between devices  19.8 us (2%)
  between operations  14.1 us (2%)
    all_to_all x1, waiting for transfers between devices, fill_ports(): return lax.all_to_all(u_next, a_name, where_dim, where_dim, tiled=True)  106 us
    all_gather x1, waiting for transfers between devices, body(): lax.all_gather(own[0][None], 'gx', axis=0, tiled=True)  79 us
    all_gather x1, waiting for transfers between devices, body(): lax.all_gather(own[1][None], 'gx', axis=0, tiled=True)  78.8 us
    all_gather x1, waiting for transfers between devices, body(): lax.all_gather(own[5][None], 'gx', axis=0, tiled=True)  78.8 us
    dynamic_slice x128, local copies, waits for them, and re-layouts, body(): prefix, _ = lax.scan(take_lower, identity, (indices, table))  75.1 us
    select_n x64, other arithmetic, take_higher(): jnp.where(keep, fresh, older)  67.8 us
    select_n x64, other arithmetic, take_lower(): jnp.where(keep, fresh, older)  67.6 us
    all_gather x1, waiting for transfers between devices, body(): lax.all_gather(own[4][None], 'gx', axis=0, tiled=True)  60.7 us
  transfers between devices with their start and end apart: 8, of which 6 were waited for; matrix products, arithmetic and copies ran while one was open for 1% of the time, Pallas kernels for 0%

profile of v1, /device:TPU:1, one launch (start us, length us, event | category | flops | bytes accessed | tf_op | source)
XLA Modules:
  0.0 791.1 jit_solution(14464908604656002919)
XLA Ops:
  8.1 1.3 collective-permute-start
  9.4 1.6 fusion.48
  11.0 1.1 slice.93
  12.1 1.2 slice.97
  13.4 6.3 fusion.32
  19.8 4.6 collective-permute-start.1
  25.8 1.4 broadcast.69.clone
  27.2 20.3 %while.64 = (s32[]{:T(128)}, f32[128,128]{1,0:T(8,128)S(1)}, f32[3,128,128]{2,1,0:T(8,128)S(1)}, f32[8,128,128]{2,1,0:T(8,128)S(1)}, f32[8,3,128,128]{3,2,1,0:T(...) while((s32[]{:T(128)}, f32[128,128]{1,0:T(8,128)S(1)}, ...), condition=%wide.region_1.2_spmd.clone, body=%wide.region_0.1_spmd.clone.sunk | while | flops 262147 | bytes 1376881 | solution.py:54
  48.5 15.2 %while.65 = (s32[]{:T(128)}, f32[3,128,128]{2,1,0:T(8,128)S(1)}, f32[8,3,128,128]{3,2,1,0:T(8,128)S(1)}, f32[8,3,128,128]{3,2,1,0:T(8,128)}, f32[8,128,128]{2,1,0:T(8,128)}, /*index=5*/s32[]{:T(128)}, s32[]{:T(128)}, s32[]{:T(128)}) while((s32[]{:T(128)}, f32[3,128,128]{2,1,0:T(8,128)S(1)}, f32[8,3,128,128]{3,2,1,0:T(8,128)S(1)}, ...), condition=%wide.region_3.4_spmd.clone, body=%wide.region_2.3_spmd.clone.sunk | while | flops 147460 | bytes 983155 | solution.py:61
  66.5 2.5 concatenate.19
  69.0 13.6 %all-to-all-start = ((f32[64,128,128]{2,1,0:T(8,128)}), f32[64,128,128]{2,1,0:T(8,128)}, u32[]{:S(2)}, u32[]{:S(2)}) async-start(f32[64,128,128]{2,1,0:T(8,128)} %concatenate.19), calls=%async_computation | async-start | bytes 8388608 | tf_op jit(solution)/shard_map/all_to_all | solution.py:13
  83.3 105.9 %all-to-all-done = f32[64,128,128]{2,1,0:T(8,128)} async-done(((f32[64,128,128]{2,1,0:T(8,128)}), f32[64,128,128]{2,1,0:T(8,128)}, u32[]{:S(2)}, u32[]{:S(2)}) %all-to-all-start) | async-done | bytes 4194336 | tf_op jit(solution)/shard_map/all_to_all | solution.py:13
  189.2 60.7 %all-gather.13.cloned.1.call-done = f32[64,1,128,128]{3,2,1,0:T(8,128)} async-done(((f32[1,1,128,128]{3,2,1,0:T(8,128)}), f32[64,1,128,128]{3,2,1,0:T(8,128)}) %all-gather.13.cloned.1.call-update) | async-done | bytes 4194320 | tf_op jit(solution)/shard_map/all_gather | solution.py:109
  249.9 79.0 %all-gather.15.cloned.1.call-done = f32[64,1,128,128]{3,2,1,0:T(8,128)} async-done(((f32[1,1,128,128]{3,2,1,0:T(8,128)}), f32[64,1,128,128]{3,2,1,0:T(8,128)}) %all-gather.15.cloned.1.call-update) | async-done | bytes 4194320 | tf_op jit(solution)/shard_map/all_gather | solution.py:105
  328.9 78.8 %all-gather.17.cloned.1.call-done = f32[64,1,128,128]{3,2,1,0:T(8,128)} async-done(((f32[1,1,128,128]{3,2,1,0:T(8,128)}), f32[64,1,128,128]{3,2,1,0:T(8,128)}) %all-gather.17.cloned.1.call-update) | async-done | bytes 4194320 | tf_op jit(solution)/shard_map/all_gather | solution.py:106
  407.7 78.8 %all-gather.19.cloned.1.call-done = f32[64,1,128,128]{3,2,1,0:T(8,128)} async-done(((f32[1,1,128,128]{3,2,1,0:T(8,128)}), f32[64,1,128,128]{3,2,1,0:T(8,128)}) %all-gather.19.cloned.1.call-update) | async-done | bytes 4194320 | tf_op jit(solution)/shard_map/all_gather | solution.py:110
  486.5 148.7 %while.67 = (s32[]{:T(128)}, f32[128,128]{1,0:T(8,128)S(1)}, f32[128,128]{1,0:T(8,128)S(1)}, s32[64]{0:T(128)S(1)}, s32[]{:T(128)}, /*index=5*/f32[64,128,128]{2...) while((s32[]{:T(128)}, f32[128,128]{1,0:T(8,128)S(1)}, ...), condition=%wide.region_7.8_spmd.clone, body=%wide.region_6.7_spmd.clone.sunk | while | flops 278533 | bytes 655541 | solution.py:128
  487.8 1.1 fusion.55
  490.1 1.1 fusion.55
  492.4 1.1 fusion.55
  494.7 1.1 fusion.55
  497.1 1.1 fusion.55
  499.4 1.1 fusion.55
  501.7 1.1 fusion.55
  504.0 1.1 fusion.55
  506.3 1.1 fusion.55
  508.7 1.1 fusion.55
  511.0 1.1 fusion.55
  513.3 1.1 fusion.55
  515.6 1.1 fusion.55
  518.0 1.1 fusion.55
  520.3 1.1 fusion.55
  522.6 1.1 fusion.55
  524.9 1.1 fusion.55
  527.3 1.1 fusion.55
  529.6 1.1 fusion.55
  531.9 1.1 fusion.55
  534.2 1.1 fusion.55
  536.5 1.1 fusion.55
  538.9 1.1 fusion.55
  541.2 1.1 fusion.55
  543.5 1.1 fusion.55
  545.8 1.1 fusion.55
  548.2 1.1 fusion.55
  550.5 1.1 fusion.55
  552.8 1.1 fusion.55
  555.1 1.1 fusion.55
  635.2 148.3 %while.66 = (s32[]{:T(128)}, f32[128,128]{1,0:T(8,128)S(1)}, f32[128,128]{1,0:T(8,128)S(1)}, s32[64]{0:T(128)S(1)}, s32[]{:T(128)}, /*index=5*/f32[64,128,128]{2...) while((s32[]{:T(128)}, f32[128,128]{1,0:T(8,128)S(1)}, ...), condition=%wide.region_5.6_spmd.clone, body=%wide.region_4.5_spmd.clone.sunk | while | flops 245764 | bytes 655521 | solution.py:127
  (316 shorter events, 221.5 us)
Async XLA Ops:
  7.2 6.2 copy-start
  7.2 6.2 copy-start.4
  7.2 6.2 copy-start.5
  7.2 182.0 %all-gather.11.cloned.1.call-start = ((), (), s32[]{:S(2)}) async-start(), calls=%async_computation.1 | async-start | bytes 4259840 | tf_op jit(solution)/shard_map/all_gather | solution.py:108
  7.2 6.2 copy-start.6
  8.1 5.2 collective-permute-start
  19.8 5.7 copy-start.1
  19.8 5.7 copy-start.2
  19.8 5.4 collective-permute-start.1
  47.5 0.8 copy-start.3
  64.5 185.5 %all-gather.13.cloned.1.call-start = ((), (), s32[]{:S(2)}) async-start(), calls=%async_computation.2 | async-start | bytes 4259840 | tf_op jit(solution)/shard_map/all_gather | solution.py:109
  65.2 263.7 %all-gather.15.cloned.1.call-start = ((), (), s32[]{:S(2)}) async-start(), calls=%async_computation.3 | async-start | bytes 4259840 | tf_op jit(solution)/shard_map/all_gather | solution.py:105
  65.9 341.8 %all-gather.17.cloned.1.call-start = ((), (), s32[]{:S(2)}) async-start(), calls=%async_computation.4 | async-start | bytes 4259840 | tf_op jit(solution)/shard_map/all_gather | solution.py:106
  69.0 120.2 %all-to-all-start = ((f32[64,128,128]{2,1,0:T(8,128)}), f32[64,128,128]{2,1,0:T(8,128)}, u32[]{:S(2)}, u32[]{:S(2)}) async-start(f32[64,128,128]{2,1,0:T(8,128)} %concatenate.19), calls=%async_computation | async-start | bytes 8388608 | tf_op jit(solution)/shard_map/all_to_all | solution.py:13
  82.7 403.8 %all-gather.19.cloned.1.call-start = ((), (), s32[]{:S(2)}) async-start(), calls=%async_computation.5 | async-start | bytes 4259840 | tf_op jit(solution)/shard_map/all_gather | solution.py:110
Sparse Core Ops, SparseCore 0:
  64.6 103.2 all-gather.10
  171.2 78.6 all-gather.12
  252.7 76.1 all-gather.14
  331.5 76.1 all-gather.16
  410.3 76.1 all-gather.18
